TPU v7x, 128 devices: a whole 4x4x4 slice. The times are simulated.
128 devices in a mesh: tm: 8 (over y, core), gx: 16 (over x, z).
Axes of the slice: x: 4, y: 4, z: 4, core: 2. Of those that a mesh axis runs over, the one named last changes fastest.
Arguments:
- end_modes: float32 [8, 256, 256, 256], P('tm', None, 'gx'), may hold values from -1 to 1
- initial_modes: float32 [256, 256, 256], P(None, 'gx'), may hold values from -1 to 1
Outputs:
- new_end_modes: float32 [8, 256, 256, 256], P('tm', None, 'gx')
- coarse_ends: float32 [8, 128, 128, 128], P('tm', None, 'gx')
All inputs are finite; a program needn't handle non-finite values.
Results may differ from a plain program's by a relative error of at most 0.00014.
Values sent between devices are 32-bit elements; how exact they have to be, the bound alone decides.
A program may use at most 128 MiB of HBM per device.

v0:
```python
import functools
import math

import jax
import jax.numpy as jnp
import ml_dtypes
import numpy as np
from jax import lax
from jax.experimental import pallas as pl
from jax.experimental.pallas import tpu as pltpu
from jax.sharding import PartitionSpec as P

F32, BF16 = jnp.float32, jnp.bfloat16
MESH = pl.DeviceIdType.MESH
GRID, COARSE, GROUPS, SLICES, BLOCK, HALF, LANES = 256, 128, 16, 8, 16, 8, 128
ROUNDS, STEP = 4, 4
DIFFUSION = 0.25
FACTOR = ((COARSE + 1) / (GRID + 1)) ** 1.5
OFFSETS = (10, 9, 11, 6, 14, 2, 8, 5, 7, 13, 15, 1, 3, 4, 12, 0)


def sine_rows(length, rows, modes):
    phase = (rows[:, None] + 1) * (modes[None, :] + 1) % (2 * (length + 1))
    return np.sin(phase * (math.pi / (length + 1))) * math.sqrt(2.0 / (length + 1))


def omega(modes, length):
    return 2.0 - 2.0 * np.cos((modes + 1.0) * (math.pi / (length + 1)))


def two(table):
    high = table.astype(ml_dtypes.bfloat16)
    rest = table - high.astype(np.float64)
    return high, rest.astype(ml_dtypes.bfloat16)


def left(table):
    high, rest = two(table)
    return np.concatenate([high, high, rest], axis=1)


def right(table):
    high, rest = two(table)
    return np.concatenate([high, rest, high], axis=0)


def tables():
    every = np.arange(GRID)
    within, group = every % BLOCK, every // BLOCK
    order = np.where(within < HALF, group * HALF + within, COARSE + group * HALF + within - HALF)
    edge = (np.arange(GROUPS) * BLOCK + np.array([[-1], [BLOCK]])).reshape(-1)
    served = every.reshape(GROUPS, ROUNDS, STEP).transpose(1, 0, 2).reshape(-1)
    edges = np.where((edge < GRID)[:, None], sine_rows(GRID, edge, every), 0.0)
    natural = sine_rows(GRID, every, every)
    permuted = sine_rows(GRID, every, order)
    fine, coarse = omega(every, GRID), omega(np.arange(COARSE), COARSE)
    wide = np.ones((1, LANES))
    as32 = lambda a: np.ascontiguousarray(a, dtype=np.float32)
    return dict(
        nat=left(natural),
        ser=left(natural[served]),
        fan=right(natural),
        per=left(permuted),
        pet=left(permuted.T),
        edg=left(edges),
        col_z=as32(DIFFUSION * fine[:, None] * wide),
        col_p=as32(DIFFUSION * fine[order][:, None] * wide),
        row_x=as32(np.broadcast_to(DIFFUSION * fine.reshape(2, 1, LANES), (2, 8, LANES))),
        col_c=as32(0.25 * DIFFUSION * coarse[:, None] * wide),
        row_c=as32(np.broadcast_to(0.25 * DIFFUSION * coarse[None, :], (8, LANES))),
        sub_c=as32(0.25 * DIFFUSION * coarse.reshape(GROUPS, HALF, 1) * wide),
        scal_p=as32(DIFFUSION * fine[order]),
        scal_c=as32(0.25 * DIFFUSION * coarse),
    )


def split(value):
    high = value.astype(BF16)
    return high, (value - high.astype(F32)).astype(BF16)


def table_times(table, value):
    high, rest = split(value)
    return jnp.dot(table, jnp.concatenate([high, rest, high], axis=0), preferred_element_type=F32)


def times_table(value, table):
    high, rest = split(value)
    return jnp.dot(jnp.concatenate([high, high, rest], axis=1), table, preferred_element_type=F32)


def reaction(field):
    return field - field * field * field


def kernel(
    end_hbm, initial_hbm, nat, ser, fan, per, pet, edg, col_z, col_p, row_x, col_c, row_c, sub_c, scal_p, scal_c,
    new, coarse,
    s_in, spread, slab, react, own, phi, base, rim_out, rim, mix_out, mix, low, low_in, ends, coarse_own, low_out,
    load_sem, in_send, in_recv, r_send, r_recv, b_send, b_recv, n_send, n_recv, l_send, l_recv,
    m_send, m_recv, e_send, e_recv, ready,
):
    t, g = lax.axis_index("tm"), lax.axis_index("gx")
    after = lax.rem(t + 1, SLICES)

    g_x, g_z = g // 4, g % 4
    along_x, along_plane = [(g_x + i) % 4 * 4 for i in range(4)], [(g_z + i) % 4 for i in range(4)]
    partners = [along_x[k // 4] + along_plane[k % 4] for k in range(GROUPS)]
    others = [lax.rem(t + k, SLICES) for k in range(SLICES)]

    def partner(k):
        return partners[k]

    def load(source, h):
        return pltpu.make_async_copy(source.at[:, :, pl.ds(h * LANES, LANES)], s_in.at[h], load_sem.at[h])

    @pl.when(t == SLICES - 1)
    def _():
        for h in range(2):
            load(initial_hbm, h).start()

    @pl.when(t != SLICES - 1)
    def _():
        for h in range(2):
            load(end_hbm.at[0], h).start()

    barrier = pltpu.get_barrier_semaphore()

    def greet(device):
        pl.semaphore_signal(barrier, inc=1, device_id=device, device_id_type=MESH)

    for k in range(1, GROUPS):
        greet((t, partner(k)))
    for k in range(1, SLICES):
        greet((others[k], g))

    def whole(plane):
        return plane.reshape(GRID, LANES)

    def two_rows(ref, y, stride):
        return jnp.concatenate([ref[pl.ds(y + i, GRID, stride=stride), :] for i in range(2)], axis=1)

    def halves(value):
        return value[:, :LANES], value[:, LANES:]

    s_rows = s_in.reshape(2, GRID * BLOCK, LANES)
    spread_rows = spread.reshape(2, GRID * BLOCK, LANES)
    own_rows = pl.multiple_of(g * BLOCK, BLOCK)

    def along_z(h, first, last):
        start, count = first * GRID // ROUNDS, (last - first) * GRID // ROUNDS

        def body(j, carry):
            value = table_times(ser[start : start + count, :], two_rows(s_rows.at[h], 2 * j, BLOCK))
            for i, half in enumerate(halves(value)):
                spread_rows[h, pl.ds(start * BLOCK + 2 * j + i, count, stride=BLOCK), :] = half
            return carry

        lax.fori_loop(0, BLOCK // 2, body, 0)

    def send_start(r, lanes):
        for k in OFFSETS[:-1]:
            to = partner(k)
            pltpu.make_async_remote_copy(
                src_ref=spread.at[lanes, r, to],
                dst_ref=slab.at[lanes, g, pl.ds(r * STEP, STEP)],
                send_sem=in_send,
                recv_sem=in_recv.at[r],
                device_id=(t, to),
                device_id_type=MESH,
            ).start()
        pltpu.make_async_copy(
            spread.at[lanes, r, g], slab.at[lanes, g, pl.ds(r * STEP, STEP)], in_recv.at[r]
        ).start()

    with jax.named_scope("ph_along0"):
        load(initial_hbm, 0).wait()
        along_z(0, 0, 1)
    with jax.named_scope("ph_barrier"):
        pl.semaphore_wait(barrier, GROUPS + SLICES - 2)
    send_start(0, pl.ds(0, 1))
    with jax.named_scope("ph_along1"):
        load(initial_hbm, 1).wait()
        along_z(1, 0, 1)
    send_start(0, pl.ds(1, 1))
    for k in range(1, SLICES):
        pl.semaphore_signal(ready, inc=1, device_id=(others[k], g), device_id_type=MESH)
    with jax.named_scope("ph_along2"):
        for h in range(2):
            along_z(h, 1, ROUNDS)
    for r in range(1, ROUNDS):
        send_start(r, pl.ds(0, 2))
    pieces = [(h, q) for h in range(2) for q in range(2)]

    couplings = (0.5 * DIFFUSION, DIFFUSION)

    def diagonal(n, octet, h):
        plane = col_p[pl.ds(octet, 8), :] + row_x[h]
        return 1.0 + 0.5 * plane + DIFFUSION if n == 0 else 1.0 + plane + 2.0 * DIFFUSION

    def ratios(n, octet, h):
        d, b = diagonal(n, octet, h), couplings[n]
        out = [b / d]
        for _ in range(BLOCK - 1):
            out.append(b / (d - b * out[-1]))
        return out

    def unit(o, carry):
        octet = pl.multiple_of(o * 8, 8)
        for n in range(2):
            for h in range(2):
                c = ratios(n, octet, h)
                v = [c[0]]
                for i in range(1, BLOCK):
                    v.append(c[i] * v[-1])
                upper = v[-1]
                phi[n, h, BLOCK - 1, pl.ds(octet, 8), :] = upper
                for i in reversed(range(BLOCK - 1)):
                    upper = v[i] + c[i] * upper
                    phi[n, h, i, pl.ds(octet, 8), :] = upper
        return carry

    with jax.named_scope("ph_unit"):
        lax.fori_loop(0, GRID // 8, unit, 0)

    def send_react(p, start, count):
        h, q = pieces[p]
        planes, places = pl.ds(start, count), pl.ds(own_rows + start, count)
        for k in OFFSETS[:-1]:
            to = partner(k)
            pltpu.make_async_remote_copy(
                src_ref=react.at[h, q, to, planes],
                dst_ref=own.at[h, q, places],
                send_sem=r_send, recv_sem=r_recv.at[p], device_id=(t, to), device_id_type=MESH,
            ).start()
        pltpu.make_async_copy(react.at[h, q, g, planes], own.at[h, q, places], r_recv.at[p]).start()

    def start_planes(j, carry):
        planes = (2 * j, 2 * j + 1)
        values = [jnp.concatenate([whole(slab[h, :, z]) for h in range(2)], axis=1) for z in planes]
        values = [table_times(per[...], value) for value in values]
        values = [reaction(times_table(value, fan[...])) for value in values]
        values = [times_table(value, fan[...]) for value in values]
        values = [table_times(pet[...], value) for value in values]
        for z, value in zip(planes, values):
            for h, half in enumerate(halves(value)):
                half = half.reshape(GROUPS, 2, 8, LANES)
                for q in range(2):
                    react[h, q, :, z] = half[:, q]
        return carry

    for r in range(ROUNDS):
        arrived = slab.at[:, :, pl.ds(r * STEP, STEP)]
        with jax.named_scope(f"ph_wait_in{r}"):
            pltpu.make_async_copy(arrived, arrived, in_recv.at[r]).wait()
        with jax.named_scope(f"ph_start{r}"):
            lax.fori_loop(r * STEP // 2, (r + 1) * STEP // 2, start_planes, 0)
        send_react(0, r * STEP, STEP)
    send_react(1, 0, BLOCK)

    def local(o, carry):
        octet = pl.multiple_of(o * 8, 8)
        here = pl.ds(octet, 8)
        for n in range(2):
            for h in range(2):
                c = ratios(n, octet, h)
                v = []
                for i in range(BLOCK):
                    right = slab[h, o // 2, i, pl.ds(o % 2 * 8, 8), :]
                    right = right + (0.5 if n == 0 else 1.0) * react[h, o % 2, o // 2, i]
                    right = right * (1.0 / couplings[n])
                    v.append(c[i] * (right + v[-1] if v else right))
                upper = v[-1]
                base[n, h, BLOCK - 1, here, :] = upper
                for i in reversed(range(BLOCK - 1)):
                    upper = v[i] + c[i] * upper
                    base[n, h, i, here, :] = upper
        return carry

    with jax.named_scope("ph_local"):
        lax.fori_loop(0, GRID // 8, local, 0)

    own_flat = own.reshape(2, 2, GRID * 8, LANES)
    rim_rows = rim_out.reshape(2, 2, GROUPS * 32, LANES)
    first = jnp.where(after == 0, FACTOR, 0.0).astype(F32)
    def in_modes(h, q, y, keep_low):
        start = two_rows(s_rows.at[h], q * 8 + y, BLOCK)
        rate = table_times(nat[...], two_rows(own_flat.at[h, q], y, 8))
        lam = jnp.concatenate(
            [col_z[...] + (row_x[h, :1, :] + scal_p[own_rows + q * 8 + y + i]) for i in range(2)], axis=1
        )
        mid = (start + 0.5 * rate) / (1.0 + 0.5 * lam)
        end = (start + rate) / (1.0 + lam)
        for i, half in enumerate(halves(end)):
            own_flat[h, q, pl.ds(y + i, GRID, stride=8), :] = half
        for n, node in enumerate((mid, end)):
            for i, half in enumerate(halves(table_times(edg[...], node))):
                for side in range(2):
                    place = pl.ds(n * 16 + side * 8 + y + i, GROUPS, stride=32)
                    rim_rows[h, q, place, :] = half[side * GROUPS : (side + 1) * GROUPS]
        if keep_low:
            for i in range(2):
                cut = lambda a: halves(a)[i][:COARSE]
                s_cut, end_cut = cut(start), cut(end)
                lam_c = col_c[...] + (row_c[:1, :] + scal_c[g * HALF + y + i])
                value = (FACTOR / 6.0) * (cut(rate) - cut(lam) * (s_cut + 4.0 * cut(mid) + end_cut))
                low[y + i] = value + lam_c * (FACTOR * end_cut) + first * s_cut

    def hand_on(p):
        h, q = pieces[p]
        kept, piece = pl.ds(COARSE, COARSE) if p == 0 else pl.ds(0, GRID), pl.ds(q * 8, 8)
        return pltpu.make_async_remote_copy(
            src_ref=own.at[h, q, kept],
            dst_ref=new.at[0, kept, piece, pl.ds(h * LANES, LANES)],
            send_sem=n_send.at[p], recv_sem=n_recv.at[p], device_id=(after, g), device_id_type=MESH,
        )

    def modes_of(p):
        h, q = pieces[p]
        here = own.at[h, q]
        with jax.named_scope(f"ph_wait_r{p}"):
            pltpu.make_async_copy(here, here, r_recv.at[p]).wait()

        def body(j, carry):
            in_modes(h, q, 2 * j, p == 0)
            return carry

        with jax.named_scope(f"ph_modes{p}"):
            lax.fori_loop(0, 4, body, 0)
        if p + 2 < len(pieces):
            send_react(p + 2, 0, BLOCK)
        for k in OFFSETS[:-1]:
            to = partner(k)
            pltpu.make_async_remote_copy(
                src_ref=rim_out.at[h, q, to],
                dst_ref=rim.at[h, g, q],
                send_sem=b_send, recv_sem=b_recv.at[h], device_id=(t, to), device_id_type=MESH,
            ).start()
        pltpu.make_async_copy(rim_out.at[h, q, g], rim.at[h, g, q], b_recv.at[h]).start()
        hand_on(p).start()
        if p == 0:
            for k in range(1, SLICES):
                to = lax.rem(t + k, SLICES)
                pltpu.make_async_remote_copy(
                    src_ref=low.at[to], dst_ref=low_in.at[after], send_sem=l_send, recv_sem=l_recv,
                    device_id=(to, g), device_id_type=MESH,
                ).start()
            pltpu.make_async_copy(low.at[t], low_in.at[after], l_recv).start()

    def nodes_on(h, z):
        return jnp.concatenate(
            [
                base[n, h, z]
                + phi[n, h, z] * whole(rim[h, :, :, n, 0])
                + phi[n, h, BLOCK - 1 - z] * whole(rim[h, :, :, n, 1])
                for n in range(2)
            ],
            axis=1,
        )

    def early(j, carry):
        for z in (2 * j, 2 * j + 1):
            for n, half in enumerate(halves(table_times(per[...], nodes_on(0, z)))):
                base[n, 0, z] = half
        return carry

    mix_rows = mix_out.reshape(COARSE * BLOCK, LANES)

    def node_planes(j, carry):
        planes = (2 * j, 2 * j + 1)
        values = [halves(table_times(per[...], nodes_on(1, z))) for z in planes]
        values = [
            [jnp.concatenate([base[n, 0, z], value[n]], axis=1) for n in range(2)]
            for z, value in zip(planes, values)
        ]
        values = [[reaction(times_table(node, fan[...])) for node in value] for value in values]
        values = [times_table(4.0 * value[0] + value[1], fan[:, :COARSE]) for value in values]
        value = table_times(nat[:COARSE, :], jnp.concatenate(values, axis=1))
        for z, half in zip(planes, halves(value)):
            mix_rows[pl.ds(z, COARSE, stride=BLOCK), :] = half
        return carry

    def rim_arrived(h):
        with jax.named_scope(f"ph_wait_rim{h}"):
            pltpu.make_async_copy(rim.at[h], rim.at[h], b_recv.at[h]).wait()

    modes_of(0)
    modes_of(1)
    modes_of(2)
    modes_of(3)
    rim_arrived(0)
    with jax.named_scope("ph_early"):
        lax.fori_loop(0, BLOCK // 2, early, 0)
    rim_arrived(1)

    def mix_source(to_t, to_g, planes):
        return mix_out.at[to_g * HALF + to_t, planes]

    def mix_place(start, count):
        return mix.at[after, pl.ds(pl.multiple_of(own_rows + start, STEP), count)]

    def send_mix(start, count, to_t, k):
        to_g = partner(k)
        pltpu.make_async_remote_copy(
            src_ref=mix_source(to_t, to_g, pl.ds(start, count)), dst_ref=mix_place(start, count),
            send_sem=m_send, recv_sem=m_recv, device_id=(to_t, to_g), device_id_type=MESH,
        ).start()

    def send_rows(start, count, first, last):
        def body(i, carry):
            to_t = lax.rem(t + i, SLICES)
            for k in OFFSETS[:-1]:
                send_mix(start, count, to_t, k)
            return carry

        lax.fori_loop(first, last, body, 0)

    def send_column(start, count):
        pltpu.make_async_copy(mix_source(t, g, pl.ds(start, count)), mix_place(start, count), m_recv).start()
        for i in range(1, SLICES):
            send_mix(start, count, others[i], 0)

    with jax.named_scope("ph_node0"):
        lax.fori_loop(0, 4, node_planes, 0)
    pl.semaphore_wait(ready, SLICES - 1)
    send_column(0, 8)
    send_rows(0, 8, 0, SLICES)

    def node_round(r, carry):
        lax.fori_loop(4 + 2 * r, 6 + 2 * r, node_planes, 0)
        start = pl.multiple_of(8 + STEP * r, STEP)
        send_column(start, STEP)
        send_rows(start, STEP, 0, SLICES)
        return carry

    with jax.named_scope("ph_node1"):
        lax.fori_loop(0, 2, node_round, 0)
    with jax.named_scope("ph_wait_mix"):
        pltpu.make_async_copy(low_in, low_in, l_recv).wait()
        pltpu.make_async_copy(mix, mix, m_recv).wait()

    with jax.named_scope("ph_scan"):
        decay = 1.0 / (1.0 + (col_c[...] + (row_c[:1, :] + scal_c[g * HALF + t])))
        current = None
        for i in range(SLICES // 2):
            value = table_times(nat[:COARSE, :], jnp.concatenate([mix[2 * i], mix[2 * i + 1]], axis=1))
            for n, half in zip((2 * i, 2 * i + 1), halves(value)):
                gain = low_in[n] + (FACTOR / 6.0) * half
                current = decay * (gain if current is None else current + gain)
                ends[n] = current
    for k in range(1, SLICES):
        to = lax.rem(t + k, SLICES)
        pltpu.make_async_remote_copy(
            src_ref=ends.at[to], dst_ref=coarse_own.at[t], send_sem=e_send, recv_sem=e_recv,
            device_id=(to, g), device_id_type=MESH,
        ).start()
    pltpu.make_async_copy(ends.at[t], coarse_own.at[t], e_recv).start()
    with jax.named_scope("ph_wait_e"):
        pltpu.make_async_copy(coarse_own, coarse_own, e_recv).wait()

    coarse_rows = coarse.reshape(COARSE * HALF, LANES)
    low_rows = low_out.reshape(COARSE * HALF, LANES)
    for j in range(HALF):
        coarse_rows[pl.ds(j, COARSE, stride=HALF), :] = coarse_own[j]
        low_rows[pl.ds(j, COARSE, stride=HALF), :] = coarse_own[j] * (1.0 / FACTOR)
    new[0, :COARSE, :HALF, :LANES] = low_out[...]

    def sent(ref, sem):
        pltpu.make_async_copy(ref, ref, sem).wait()

    with jax.named_scope("ph_drain"):
        sent(spread.at[:, :, pl.ds(0, GROUPS - 1)], in_send)
        sent(react.at[:, :, pl.ds(0, GROUPS - 1)], r_send)
        sent(rim_out.at[:, :, pl.ds(0, GROUPS - 1)], b_send)
        sent(low.at[pl.ds(0, SLICES - 1)], l_send)
        sent(mix_out.at[pl.ds(0, COARSE - 1)], m_send)
        sent(ends.at[pl.ds(0, SLICES - 1)], e_send)
        for p in range(len(pieces)):
            hand_on(p).wait()


def solution(mesh):
    vmem = pl.BlockSpec(memory_space=pltpu.VMEM)
    hbm = pl.BlockSpec(memory_space=pl.ANY)
    smem = pl.BlockSpec(memory_space=pltpu.SMEM)
    held = tables()

    def per_device(end_modes, initial_modes):
        slab = (2, BLOCK, GRID, LANES)
        coarse = (COARSE, HALF, LANES)
        share = (SLICES, COARSE, LANES)
        dma = pltpu.SemaphoreType.DMA
        scratch = [
            (2, GRID, BLOCK, LANES), (2, ROUNDS, GROUPS, STEP, BLOCK, LANES), (2, GROUPS, BLOCK, BLOCK, LANES),
            (2, 2, GROUPS, BLOCK, 8, LANES), (2, 2, GRID, 8, LANES), (2, *slab), (2, *slab),
            (2, 2, GROUPS, 2, 2, 8, LANES), (2, GROUPS, 2, 2, 2, 8, LANES),
            (COARSE, BLOCK, LANES), (SLICES, GRID, LANES), share, share, share, share, coarse,
        ]
        counts = [2, 0, ROUNDS, 0, 4, 0, 2, 4, 4, 0, 0, 0, 0, 0, 0]
        sems = [dma((n,)) if n else dma for n in counts] + [pltpu.SemaphoreType.REGULAR]
        return pl.pallas_call(
            kernel,
            name="pfasst",
            out_shape=(
                pltpu.VMEM(end_modes.shape, F32),
                pltpu.VMEM((1, *coarse), F32),
            ),
            in_specs=[hbm, hbm] + [vmem] * 12 + [smem] * 2,
            out_specs=(vmem, vmem),
            scratch_shapes=[pltpu.VMEM(s, F32) for s in scratch] + sems,
            compiler_params=pltpu.CompilerParams(collective_id=0, has_side_effects=True, vmem_limit_bytes=54 << 20),
        )(end_modes, initial_modes, *held.values())

    return jax.shard_map(
        per_device,
        mesh=mesh,
        in_specs=(P("tm", None, "gx", None), P(None, "gx", None)),
        out_specs=(P("tm", None, "gx", None), P("tm", None, "gx", None)),
        check_vma=False,
    )
```

profile of v0, /device:TPU:1, one launch (start us, length us, event | category | flops | bytes accessed | tf_op | source)
XLA Modules:
  0.0 150.7 jit_solution(9345025398167285086)
XLA Ops:
  0.6 147.3 %pfasst.1 = (f32[1,256,16,256]{3,2,1,0:T(8,128)S(1)}, f32[1,128,8,128]{3,2,1,0:T(8,128)S(1)}) custom-call(f32[1,256,16,256]{3,2,1,0:T(8,128)} %end_hbm.1, f32[256,16,256]{2,1,0:T(8,128)} %initial_hbm.1, bf16[256,768]{1,0:T(8,128)(2,1)} %constant.28.clone.nat, bf16[256,768]{1,0:T(8,128)(2,1)} %constant.29.clone.ser, bf16[768,256]{1,0:T(8,128)(2,1)} %constant.30.clone.fan, ...), custom_call_target="tpu_custom_call" | custom-call | tf_op jit(solution)/shard_map/pfasst/pallas_call | solution.py:501
  147.9 2.0 %copy.20 = f32[1,256,16,256]{3,2,1,0:T(8,128)} copy(f32[1,256,16,256]{3,2,1,0:T(8,128)S(1)} %get-tuple-element.2) | data formatting | bytes 8388608
  150.0 0.8 copy.21
where the time goes:
time: 151 us
  Pallas kernels  147 us (97%)
  local copies, waits for them, and re-layouts  2.81 us (2%)
    pallas_call x1, Pallas kernels, per_device(): pl.pallas_call(kernel, name='pfasst', out_shape=(pltpu.VMEM(end_modes.sha...  147 us

commit v1 on v0

--- a/solution.py
+++ b/solution.py
@@ -17,6 +17,9 @@
 DIFFUSION = 0.25
 FACTOR = ((COARSE + 1) / (GRID + 1)) ** 1.5
 OFFSETS = (10, 9, 11, 6, 14, 2, 8, 5, 7, 13, 15, 1, 3, 4, 12, 0)
+
+
+FAR_FIRST = (4, 3, 5, 2, 6, 1, 7)
 
 
 def sine_rows(length, rows, modes):
@@ -96,7 +99,7 @@
 def kernel(
     end_hbm, initial_hbm, nat, ser, fan, per, pet, edg, col_z, col_p, row_x, col_c, row_c, sub_c, scal_p, scal_c,
     new, coarse,
-    s_in, spread, slab, react, own, phi, base, rim_out, rim, mix_out, mix, low, low_in, ends, coarse_own, low_out,
+    s_in, spread, slab, react, own, phi, base, rim_out, rim, mix_out, mix, low, low_in, ends, coarse_own, low_out, inverse,
     load_sem, in_send, in_recv, r_send, r_recv, b_send, b_recv, n_send, n_recv, l_send, l_recv,
     m_send, m_recv, e_send, e_recv, ready,
 ):
@@ -114,15 +117,16 @@
     def load(source, h):
         return pltpu.make_async_copy(source.at[:, :, pl.ds(h * LANES, LANES)], s_in.at[h], load_sem.at[h])
 
-    @pl.when(t == SLICES - 1)
-    def _():
-        for h in range(2):
+    def start_load(h):
+        @pl.when(t == SLICES - 1)
+        def _():
             load(initial_hbm, h).start()
 
-    @pl.when(t != SLICES - 1)
-    def _():
-        for h in range(2):
+        @pl.when(t != SLICES - 1)
+        def _():
             load(end_hbm.at[0], h).start()
+
+    start_load(0)
 
     barrier = pltpu.get_barrier_semaphore()
 
@@ -175,6 +179,7 @@
 
     with jax.named_scope("ph_along0"):
         load(initial_hbm, 0).wait()
+        start_load(1)
         along_z(0, 0, 1)
     with jax.named_scope("ph_barrier"):
         pl.semaphore_wait(barrier, GROUPS + SLICES - 2)
@@ -283,14 +288,16 @@
     own_flat = own.reshape(2, 2, GRID * 8, LANES)
     rim_rows = rim_out.reshape(2, 2, GROUPS * 32, LANES)
     first = jnp.where(after == 0, FACTOR, 0.0).astype(F32)
+    def eigen(h, q, y):
+        return jnp.concatenate(
+            [col_z[...] + (row_x[h, :1, :] + scal_p[own_rows + q * 8 + y + i]) for i in range(2)], axis=1
+        )
+
     def in_modes(h, q, y, keep_low):
         start = two_rows(s_rows.at[h], q * 8 + y, BLOCK)
         rate = table_times(nat[...], two_rows(own_flat.at[h, q], y, 8))
-        lam = jnp.concatenate(
-            [col_z[...] + (row_x[h, :1, :] + scal_p[own_rows + q * 8 + y + i]) for i in range(2)], axis=1
-        )
-        mid = (start + 0.5 * rate) / (1.0 + 0.5 * lam)
-        end = (start + rate) / (1.0 + lam)
+        mid = (start + 0.5 * rate) * inverse[0, y // 2]
+        end = (start + rate) * inverse[1, y // 2]
         for i, half in enumerate(halves(end)):
             own_flat[h, q, pl.ds(y + i, GRID, stride=8), :] = half
         for n, node in enumerate((mid, end)):
@@ -299,6 +306,7 @@
                     place = pl.ds(n * 16 + side * 8 + y + i, GROUPS, stride=32)
                     rim_rows[h, q, place, :] = half[side * GROUPS : (side + 1) * GROUPS]
         if keep_low:
+            lam = eigen(h, q, y)
             for i in range(2):
                 cut = lambda a: halves(a)[i][:COARSE]
                 s_cut, end_cut = cut(start), cut(end)
@@ -318,6 +326,14 @@
     def modes_of(p):
         h, q = pieces[p]
         here = own.at[h, q]
+
+        def invert(j, carry):
+            lam = eigen(h, q, 2 * j)
+            inverse[0, j] = 1.0 / (1.0 + 0.5 * lam)
+            inverse[1, j] = 1.0 / (1.0 + lam)
+            return carry
+
+        lax.fori_loop(0, 4, invert, 0)
         with jax.named_scope(f"ph_wait_r{p}"):
             pltpu.make_async_copy(here, here, r_recv.at[p]).wait()
 
@@ -374,10 +390,10 @@
             for z, value in zip(planes, values)
         ]
         values = [[reaction(times_table(node, fan[...])) for node in value] for value in values]
-        values = [times_table(4.0 * value[0] + value[1], fan[:, :COARSE]) for value in values]
-        value = table_times(nat[:COARSE, :], jnp.concatenate(values, axis=1))
-        for z, half in zip(planes, halves(value)):
-            mix_rows[pl.ds(z, COARSE, stride=BLOCK), :] = half
+        values = [table_times(nat[:COARSE, :], 4.0 * value[0] + value[1]) for value in values]
+        value = times_table(jnp.concatenate(values, axis=0), fan[:, :COARSE])
+        for i, z in enumerate(planes):
+            mix_rows[pl.ds(z, COARSE, stride=BLOCK), :] = value[i * COARSE : (i + 1) * COARSE]
         return carry
 
     def rim_arrived(h):
@@ -408,7 +424,7 @@
 
     def send_rows(start, count, first, last):
         def body(i, carry):
-            to_t = lax.rem(t + i, SLICES)
+            to_t = lax.rem(t + 4 + (i + 1) // 2 * (1 - 2 * (i % 2)), SLICES)
             for k in OFFSETS[:-1]:
                 send_mix(start, count, to_t, k)
             return carry
@@ -417,20 +433,20 @@
 
     def send_column(start, count):
         pltpu.make_async_copy(mix_source(t, g, pl.ds(start, count)), mix_place(start, count), m_recv).start()
-        for i in range(1, SLICES):
+        for i in FAR_FIRST:
             send_mix(start, count, others[i], 0)
 
     with jax.named_scope("ph_node0"):
         lax.fori_loop(0, 4, node_planes, 0)
     pl.semaphore_wait(ready, SLICES - 1)
+    send_rows(0, 8, 0, SLICES)
     send_column(0, 8)
-    send_rows(0, 8, 0, SLICES)
 
     def node_round(r, carry):
         lax.fori_loop(4 + 2 * r, 6 + 2 * r, node_planes, 0)
         start = pl.multiple_of(8 + STEP * r, STEP)
+        send_rows(start, STEP, 0, SLICES)
         send_column(start, STEP)
-        send_rows(start, STEP, 0, SLICES)
         return carry
 
     with jax.named_scope("ph_node1"):
@@ -448,8 +464,8 @@
                 gain = low_in[n] + (FACTOR / 6.0) * half
                 current = decay * (gain if current is None else current + gain)
                 ends[n] = current
-    for k in range(1, SLICES):
-        to = lax.rem(t + k, SLICES)
+    for k in FAR_FIRST:
+        to = others[k]
         pltpu.make_async_remote_copy(
             src_ref=ends.at[to], dst_ref=coarse_own.at[t], send_sem=e_send, recv_sem=e_recv,
             device_id=(to, g), device_id_type=MESH,
@@ -494,7 +510,7 @@
             (2, GRID, BLOCK, LANES), (2, ROUNDS, GROUPS, STEP, BLOCK, LANES), (2, GROUPS, BLOCK, BLOCK, LANES),
             (2, 2, GROUPS, BLOCK, 8, LANES), (2, 2, GRID, 8, LANES), (2, *slab), (2, *slab),
             (2, 2, GROUPS, 2, 2, 8, LANES), (2, GROUPS, 2, 2, 2, 8, LANES),
-            (COARSE, BLOCK, LANES), (SLICES, GRID, LANES), share, share, share, share, coarse,
+            (COARSE, BLOCK, LANES), (SLICES, GRID, LANES), share, share, share, share, coarse, (2, 4, GRID, GRID),
         ]
         counts = [2, 0, ROUNDS, 0, 4, 0, 2, 4, 4, 0, 0, 0, 0, 0, 0]
         sems = [dma((n,)) if n else dma for n in counts] + [pltpu.SemaphoreType.REGULAR]

time: 151 us -> 149 us (0.987)
  Pallas kernels: 147 us -> 145 us
    pallas_call x1, Pallas kernels: 147 us -> 145 us  [per_device(): pl.pallas_call(kernel, name='pfasst', out_shape=(pltpu.VMEM(end_modes.sha...]
where the time goes in v1:
time: 149 us
  Pallas kernels  145 us (97%)
  local copies, waits for them, and re-layouts  2.81 us (2%)
    pallas_call x1, Pallas kernels, per_device(): pl.pallas_call(kernel, name='pfasst', out_shape=(pltpu.VMEM(end_modes.sha...  145 us

profile of v1, /device:TPU:1, one launch (start us, length us, event | category | flops | bytes accessed | tf_op | source)
XLA Modules:
  0.0 148.7 jit_solution(17179421403572232633)
XLA Ops:
  0.6 145.2 %pfasst.1 = (f32[1,256,16,256]{3,2,1,0:T(8,128)S(1)}, f32[1,128,8,128]{3,2,1,0:T(8,128)S(1)}) custom-call(f32[1,256,16,256]{3,2,1,0:T(8,128)} %end_hbm.1, f32[256,16,256]{2,1,0:T(8,128)} %initial_hbm.1, bf16[256,768]{1,0:T(8,128)(2,1)} %constant.28.clone.nat, bf16[256,768]{1,0:T(8,128)(2,1)} %constant.29.clone.ser, bf16[768,256]{1,0:T(8,128)(2,1)} %constant.30.clone.fan, ...), custom_call_target="tpu_custom_call" | custom-call | tf_op jit(solution)/shard_map/pfasst/pallas_call | solution.py:517
  145.9 2.0 %copy.20 = f32[1,256,16,256]{3,2,1,0:T(8,128)} copy(f32[1,256,16,256]{3,2,1,0:T(8,128)S(1)} %get-tuple-element.2) | data formatting | bytes 8388608
  147.9 0.8 copy.21
